TPU v7x, 128 devices: a whole 4x4x4 slice. The times are simulated.
128 devices in a mesh: query: 8 (over x, z_hi), tok: 16 (over y, z_lo, core).
Axes of the slice: x: 4, y: 4, z: 4 (z_hi: 2, z_lo: 2; z = z_hi * 2 + z_lo), core: 2. Of those that a mesh axis runs over, the one named last changes fastest.
Arguments:
- queries: bfloat16 [32768, 128], P('query'), may hold values from -16 to 16, as said below
- documents: bfloat16 [32768, 128], P('tok'), may hold values from -10 to 10, as said below
- cotangent: float32 [1024], P('query'), may hold values from -6 to 6
Outputs:
- grad_queries: float32 [32768, 128], P(('query', 'tok'))
- grad_documents: float32 [16, 2048, 128], P('tok', 'query')
Inputs may be any that keep to these rules, and one draw needn't show every extreme that they name: `documents`: document embeddings of order one. `queries`: query embeddings of order one.
All inputs are finite; a program needn't handle non-finite values.
Results may differ from a plain program's by a relative error of at most 0.0029.
Values may be sent and summed in bfloat16 or wider, within the bound.
A program may use at most 64 MiB of HBM per device.

v0:
```python
import jax
import jax.numpy as jnp
from jax import lax
from jax.sharding import PartitionSpec as P

QLEN = 32
inv_temp = 2.0


def score_rows(q_rows, doc_rows):
    return (
        lax.dot_general(
            q_rows, doc_rows, (((1,), (1,)), ((), ())), preferred_element_type=jnp.float32
        )
        * inv_temp
    )


def shards(queries, documents, cotangent):
    n_rows, feat_width = queries.shape
    n_docs = documents.shape[0]
    blk_rows = min(512, n_rows)
    n_blocks = n_rows // blk_rows
    row_weight = jnp.broadcast_to(cotangent[:, None], (cotangent.shape[0], QLEN)).reshape(-1)
    q_blocks = queries.reshape(n_blocks, blk_rows, feat_width)

    def local_stats(carry, q_rows):
        scores = score_rows(q_rows, documents)
        row_top = jnp.max(scores, axis=1)
        row_total = jnp.sum(jnp.exp(scores - row_top[:, None]), axis=1)
        return (carry, (row_top, row_total))

    _, (row_tops, row_totals) = lax.scan(local_stats, 0, q_blocks)
    row_tops = row_tops.reshape(-1)
    row_totals = row_totals.reshape(-1)
    top_all = lax.pmax(row_tops, "tok")
    total_all = lax.psum(row_totals * jnp.exp(row_tops - top_all), "tok")
    log_total = top_all + jnp.log(total_all)
    log_blocks = log_total.reshape(n_blocks, blk_rows)
    weight_blocks = row_weight.reshape(n_blocks, blk_rows)

    def backward_both(doc_total, inputs_blk):
        q_rows, log_rows, weight_rows = inputs_blk
        scores = score_rows(q_rows, documents)
        probs = jnp.exp(scores - log_rows[:, None])
        weights_low = probs.astype(jnp.bfloat16)
        grad_rows = weight_rows[:, None] * jnp.dot(
            weights_low, documents, preferred_element_type=jnp.float32
        )
        scaled = (weight_rows[:, None] * probs).astype(jnp.bfloat16)
        doc_total = doc_total + lax.dot_general(
            scaled, q_rows, (((0,), (0,)), ((), ())), preferred_element_type=jnp.float32
        )
        return (doc_total, grad_rows)

    doc_total, grad_blocks = lax.scan(
        backward_both,
        jnp.zeros((n_docs, feat_width), jnp.float32),
        (q_blocks, log_blocks, weight_blocks),
    )
    grad_docs = lax.psum_scatter(doc_total, "query", scatter_dimension=0, tiled=True)
    query_terms = grad_blocks.reshape(n_rows, feat_width)
    grad_q = lax.psum_scatter(query_terms, "tok", scatter_dimension=0, tiled=True)
    return (grad_q, grad_docs[None])


def solution(mesh):
    placed = (P("query", None), P("tok", None), P("query"))
    return jax.shard_map(
        shards,
        mesh=mesh,
        in_specs=placed,
        out_specs=(P(("query", "tok"), None), P("tok", "query", None)),
        check_vma=False,
    )
```

profile of v0, /device:TPU:0, one launch (start us, length us, event | category | flops | bytes accessed | tf_op | source)
XLA Modules:
  0.0 358.9 jit_solution(10717387732099525368)
XLA Ops:
  7.3 23.1 %while.25 = (s32[]{:T(128)}, f32[8,512]{1,0:T(8,128)S(1)}, f32[8,512]{1,0:T(8,128)S(1)}, bf16[8,512,128]{2,1,0:T(8,128)(2,1)}, bf16[2048,128]{1,0:T(8,128)(2,1)}, /*index=5*/s32[]{:T(128)}, s32[]{:T(128)}) while((s32[]{:T(128)}, f32[8,512]{1,0:T(8,128)S(1)}, f32[8,512]{1,0:T(8,128)S(1)}, bf16[8,512,128]{2,1,0:T(8,128)(2,1)}, ...), condition=%wide.region_3.4_spmd, body=%wide.region_0.3_spmd.sunk | while | flops 273677312 | bytes 9058901 | solution.py:33
  7.3 1.9 multiply_reduce_fusion.2
  9.2 0.8 exponential_reduce_fusion.2
  10.1 0.1 dynamic_update_slice.16
  10.2 1.9 multiply_reduce_fusion.2
  12.1 0.8 exponential_reduce_fusion.2
  12.9 0.1 dynamic_update_slice.16
  13.0 1.9 multiply_reduce_fusion.2
  14.9 0.8 exponential_reduce_fusion.2
  15.8 0.1 dynamic_update_slice.16
  15.9 1.9 multiply_reduce_fusion.2
  17.8 0.8 exponential_reduce_fusion.2
  18.7 0.1 dynamic_update_slice.16
  18.8 1.9 multiply_reduce_fusion.2
  20.7 0.8 exponential_reduce_fusion.2
  21.7 1.9 multiply_reduce_fusion.2
  23.6 0.8 exponential_reduce_fusion.2
  24.5 0.1 dynamic_update_slice.16
  24.6 1.9 multiply_reduce_fusion.2
  26.5 0.8 exponential_reduce_fusion.2
  27.4 1.9 multiply_reduce_fusion.2
  29.4 0.8 exponential_reduce_fusion.2
  30.3 56.7 %pmax.7 = f32[4096]{0:T(1024)S(1)} all-reduce(f32[4096]{0:T(1024)S(1)} %bitcast.57), channel_id=1, replica_groups=mesh['query'=8,'tok'=16] {'tok'}, use_global_device_ids=true, to_apply=%region_4.5 | all-reduce | flops 4096 | bytes 32768 | tf_op jit(solution)/shard_map/pmax | solution.py:36
  87.0 52.9 %psum.7 = f32[4096]{0:T(1024)S(1)} all-reduce(f32[4096]{0:T(1024)S(1)} %exponential_multiply_fusion), channel_id=1, replica_groups=mesh['query'=8,'tok'=16] {'tok'}, use_global_device_ids=true, to_apply=%region_5.6 | all-reduce | flops 4096 | bytes 32768 | tf_op jit(solution)/shard_map/psum | solution.py:37
  139.9 0.1 broadcast_in_dim.36
  140.0 0.1 broadcast_in_dim.37
  140.1 0.1 broadcast_in_dim.38
  140.2 72.0 %while.26 = (s32[]{:T(128)}, f32[2048,128]{1,0:T(8,128)S(1)}, f32[8,512,128]{2,1,0:T(8,128)}, f32[8,512]{1,0:T(8,128)S(1)}, bf16[8,512,128]{2,1,0:T(8,128)(2,1)}...) while((s32[]{:T(128)}, f32[2048,128]{1,0:T(8,128)S(1)}, ...), condition=%wide.region_7.8_spmd.clone, body=%wide.region_6.7_spmd.clone.sunk | while | flops 813236224 | bytes 35145376 | solution.py:56
  140.2 1.9 fusion.46
  142.1 1.9 copy-done
  144.0 1.5 fusion.47
  145.6 3.6 %convolution_add_fusion.2 = f32[2048,128]{1,0:T(8,128)S(1)} fusion(f32[512,2048]{1,0:T(8,128)} %copy-done, f32[512]{0:T(512)S(1)} %bitcast.53, f32[512]{0:T(512)S(1)} %bitcast.55, f32[2048,128]{1,0:T(8,128)S(1)} %get-tuple-element.237, pred[]{:T(512)S(6)} %compare.3, bf16[8,512,128]{2,1,0:T(8,128)(2,1)} %get-tuple-element.249, s32[]{:T(128)} %get-tuple-element.236), kind=kOutput, calls=%fused_computation.9.clone.1 | convolution fusion | flops 273154048 | bytes 6427137 | tf_op jit(solution)/shard_map/while/body/eval_jaxpr/dot_general | solution.py:51
  149.2 1.9 fusion.46
  151.1 1.9 copy-done
  153.0 1.5 fusion.47
  154.6 3.6 %convolution_add_fusion.2 = f32[2048,128]{1,0:T(8,128)S(1)} fusion(f32[512,2048]{1,0:T(8,128)} %copy-done, f32[512]{0:T(512)S(1)} %bitcast.53, f32[512]{0:T(512)S(1)} %bitcast.55, f32[2048,128]{1,0:T(8,128)S(1)} %get-tuple-element.237, pred[]{:T(512)S(6)} %compare.3, bf16[8,512,128]{2,1,0:T(8,128)(2,1)} %get-tuple-element.249, s32[]{:T(128)} %get-tuple-element.236), kind=kOutput, calls=%fused_computation.9.clone.1 | convolution fusion | flops 273154048 | bytes 6427137 | tf_op jit(solution)/shard_map/while/body/eval_jaxpr/dot_general | solution.py:51
  158.2 1.9 fusion.46
  160.1 1.9 copy-done
  162.0 1.6 fusion.47
  163.6 3.6 %convolution_add_fusion.2 = f32[2048,128]{1,0:T(8,128)S(1)} fusion(f32[512,2048]{1,0:T(8,128)} %copy-done, f32[512]{0:T(512)S(1)} %bitcast.53, f32[512]{0:T(512)S(1)} %bitcast.55, f32[2048,128]{1,0:T(8,128)S(1)} %get-tuple-element.237, pred[]{:T(512)S(6)} %compare.3, bf16[8,512,128]{2,1,0:T(8,128)(2,1)} %get-tuple-element.249, s32[]{:T(128)} %get-tuple-element.236), kind=kOutput, calls=%fused_computation.9.clone.1 | convolution fusion | flops 273154048 | bytes 6427137 | tf_op jit(solution)/shard_map/while/body/eval_jaxpr/dot_general | solution.py:51
  167.2 1.9 fusion.46
  169.1 1.9 copy-done
  171.0 1.6 fusion.47
  172.6 3.6 %convolution_add_fusion.2 = f32[2048,128]{1,0:T(8,128)S(1)} fusion(f32[512,2048]{1,0:T(8,128)} %copy-done, f32[512]{0:T(512)S(1)} %bitcast.53, f32[512]{0:T(512)S(1)} %bitcast.55, f32[2048,128]{1,0:T(8,128)S(1)} %get-tuple-element.237, pred[]{:T(512)S(6)} %compare.3, bf16[8,512,128]{2,1,0:T(8,128)(2,1)} %get-tuple-element.249, s32[]{:T(128)} %get-tuple-element.236), kind=kOutput, calls=%fused_computation.9.clone.1 | convolution fusion | flops 273154048 | bytes 6427137 | tf_op jit(solution)/shard_map/while/body/eval_jaxpr/dot_general | solution.py:51
  176.2 1.9 fusion.46
  178.1 1.9 copy-done
  180.0 1.5 fusion.47
  181.6 3.6 %convolution_add_fusion.2 = f32[2048,128]{1,0:T(8,128)S(1)} fusion(f32[512,2048]{1,0:T(8,128)} %copy-done, f32[512]{0:T(512)S(1)} %bitcast.53, f32[512]{0:T(512)S(1)} %bitcast.55, f32[2048,128]{1,0:T(8,128)S(1)} %get-tuple-element.237, pred[]{:T(512)S(6)} %compare.3, bf16[8,512,128]{2,1,0:T(8,128)(2,1)} %get-tuple-element.249, s32[]{:T(128)} %get-tuple-element.236), kind=kOutput, calls=%fused_computation.9.clone.1 | convolution fusion | flops 273154048 | bytes 6427137 | tf_op jit(solution)/shard_map/while/body/eval_jaxpr/dot_general | solution.py:51
  185.2 1.9 fusion.46
  187.1 1.9 copy-done
  189.0 1.6 fusion.47
  190.6 3.6 %convolution_add_fusion.2 = f32[2048,128]{1,0:T(8,128)S(1)} fusion(f32[512,2048]{1,0:T(8,128)} %copy-done, f32[512]{0:T(512)S(1)} %bitcast.53, f32[512]{0:T(512)S(1)} %bitcast.55, f32[2048,128]{1,0:T(8,128)S(1)} %get-tuple-element.237, pred[]{:T(512)S(6)} %compare.3, bf16[8,512,128]{2,1,0:T(8,128)(2,1)} %get-tuple-element.249, s32[]{:T(128)} %get-tuple-element.236), kind=kOutput, calls=%fused_computation.9.clone.1 | convolution fusion | flops 273154048 | bytes 6427137 | tf_op jit(solution)/shard_map/while/body/eval_jaxpr/dot_general | solution.py:51
  194.2 1.9 fusion.46
  196.1 1.9 copy-done
  198.0 1.6 fusion.47
  199.6 3.6 %convolution_add_fusion.2 = f32[2048,128]{1,0:T(8,128)S(1)} fusion(f32[512,2048]{1,0:T(8,128)} %copy-done, f32[512]{0:T(512)S(1)} %bitcast.53, f32[512]{0:T(512)S(1)} %bitcast.55, f32[2048,128]{1,0:T(8,128)S(1)} %get-tuple-element.237, pred[]{:T(512)S(6)} %compare.3, bf16[8,512,128]{2,1,0:T(8,128)(2,1)} %get-tuple-element.249, s32[]{:T(128)} %get-tuple-element.236), kind=kOutput, calls=%fused_computation.9.clone.1 | convolution fusion | flops 273154048 | bytes 6427137 | tf_op jit(solution)/shard_map/while/body/eval_jaxpr/dot_general | solution.py:51
  203.2 1.9 fusion.46
  205.1 1.9 copy-done
  207.0 1.6 fusion.47
  208.6 3.6 %convolution_add_fusion.2 = f32[2048,128]{1,0:T(8,128)S(1)} fusion(f32[512,2048]{1,0:T(8,128)} %copy-done, f32[512]{0:T(512)S(1)} %bitcast.53, f32[512]{0:T(512)S(1)} %bitcast.55, f32[2048,128]{1,0:T(8,128)S(1)} %get-tuple-element.237, pred[]{:T(512)S(6)} %compare.3, bf16[8,512,128]{2,1,0:T(8,128)(2,1)} %get-tuple-element.249, s32[]{:T(128)} %get-tuple-element.236), kind=kOutput, calls=%fused_computation.9.clone.1 | convolution fusion | flops 273154048 | bytes 6427137 | tf_op jit(solution)/shard_map/while/body/eval_jaxpr/dot_general | solution.py:51
  212.2 1.0 copy-done.2
  213.3 0.7 reduce-scatter.3.cloned.1.call-update
  214.0 71.5 %reduce-scatter.5.cloned.1.call-done = f32[256,128]{1,0:T(8,128)} async-done(((f32[2048,128]{1,0:T(8,128)}), f32[256,128]{1,0:T(8,128)}) %reduce-scatter.5.cloned.1.call-update) | async-done | bytes 131088 | tf_op jit(solution)/shard_map/reduce_scatter | solution.py:61
  285.5 66.6 %reduce-scatter.3.cloned.1.call-done = f32[256,128]{1,0:T(8,128)} async-done(((f32[4096,128]{1,0:T(8,128)}), f32[256,128]{1,0:T(8,128)}) %reduce-scatter.3.cloned.1.call-update) | async-done | bytes 131088 | tf_op jit(solution)/shard_map/reduce_scatter | solution.py:63
  (58 shorter events, 1.0 us)
Async XLA Ops:
  7.2 278.3 %reduce-scatter.5.cloned.1.call-start = ((), (), s32[]{:S(2)}) async-start(), calls=%async_computation.3 | async-start | bytes 1179648 | tf_op jit(solution)/shard_map/reduce_scatter | solution.py:61
  7.2 132.7 %copy-start.3 = (f32[128]{0:T(128)S(1)}, f32[128]{0:T(128)}, u32[]{:S(2)}) copy-start(f32[128]{0:T(128)} %param.9) | copy-start | bytes 1540
  140.2 3.8 %copy-start.1 = (bf16[2048,128]{1,0:T(8,128)(2,1)S(1)}, bf16[2048,128]{1,0:T(8,128)(2,1)}, u32[]{:S(2)}) copy-start(bf16[2048,128]{1,0:T(8,128)(2,1)} %get-tuple-element.250) | copy-start | bytes 1572868 | tf_op jit(solution)/shard_map/while
  142.1 1.9 copy-start
  149.2 3.8 %copy-start.1 = (bf16[2048,128]{1,0:T(8,128)(2,1)S(1)}, bf16[2048,128]{1,0:T(8,128)(2,1)}, u32[]{:S(2)}) copy-start(bf16[2048,128]{1,0:T(8,128)(2,1)} %get-tuple-element.250) | copy-start | bytes 1572868 | tf_op jit(solution)/shard_map/while
  151.1 1.9 copy-start
  158.2 3.8 %copy-start.1 = (bf16[2048,128]{1,0:T(8,128)(2,1)S(1)}, bf16[2048,128]{1,0:T(8,128)(2,1)}, u32[]{:S(2)}) copy-start(bf16[2048,128]{1,0:T(8,128)(2,1)} %get-tuple-element.250) | copy-start | bytes 1572868 | tf_op jit(solution)/shard_map/while
  160.1 1.9 copy-start
  167.2 3.8 %copy-start.1 = (bf16[2048,128]{1,0:T(8,128)(2,1)S(1)}, bf16[2048,128]{1,0:T(8,128)(2,1)}, u32[]{:S(2)}) copy-start(bf16[2048,128]{1,0:T(8,128)(2,1)} %get-tuple-element.250) | copy-start | bytes 1572868 | tf_op jit(solution)/shard_map/while
  169.1 1.9 copy-start
  176.2 3.8 %copy-start.1 = (bf16[2048,128]{1,0:T(8,128)(2,1)S(1)}, bf16[2048,128]{1,0:T(8,128)(2,1)}, u32[]{:S(2)}) copy-start(bf16[2048,128]{1,0:T(8,128)(2,1)} %get-tuple-element.250) | copy-start | bytes 1572868 | tf_op jit(solution)/shard_map/while
  178.1 1.9 copy-start
  185.2 3.8 %copy-start.1 = (bf16[2048,128]{1,0:T(8,128)(2,1)S(1)}, bf16[2048,128]{1,0:T(8,128)(2,1)}, u32[]{:S(2)}) copy-start(bf16[2048,128]{1,0:T(8,128)(2,1)} %get-tuple-element.250) | copy-start | bytes 1572868 | tf_op jit(solution)/shard_map/while
  187.1 1.9 copy-start
  194.2 3.8 %copy-start.1 = (bf16[2048,128]{1,0:T(8,128)(2,1)S(1)}, bf16[2048,128]{1,0:T(8,128)(2,1)}, u32[]{:S(2)}) copy-start(bf16[2048,128]{1,0:T(8,128)(2,1)} %get-tuple-element.250) | copy-start | bytes 1572868 | tf_op jit(solution)/shard_map/while
  196.1 1.9 copy-start
  203.2 3.8 %copy-start.1 = (bf16[2048,128]{1,0:T(8,128)(2,1)S(1)}, bf16[2048,128]{1,0:T(8,128)(2,1)}, u32[]{:S(2)}) copy-start(bf16[2048,128]{1,0:T(8,128)(2,1)} %get-tuple-element.250) | copy-start | bytes 1572868 | tf_op jit(solution)/shard_map/while
  205.1 1.9 copy-start
  212.2 1.0 copy-start.2
  213.2 138.9 %reduce-scatter.3.cloned.1.call-start = ((), (), s32[]{:S(2)}) async-start(), calls=%async_computation.2 | async-start | bytes 2228224 | tf_op jit(solution)/shard_map/reduce_scatter | solution.py:63
Sparse Core Ops, SparseCore 0:
  213.4 72.0 reduce-scatter.4
  288.4 63.6 reduce-scatter.2
where the time goes:
time: 359 us
  waiting for transfers between devices  139 us (39%)
  blocking collectives  110 us (31%)
  matrix products  71.5 us (20%)
  local copies, waits for them, and re-layouts  17.5 us (5%)
  between operations  14.1 us (4%)
  other arithmetic  6.62 us (2%)
    reduce_scatter x1, waiting for transfers between devices, shards(): lax.psum_scatter(doc_total, 'query', scatter_dimension=0, tiled=True)  71.5 us
    reduce_scatter x1, waiting for transfers between devices, shards(): lax.psum_scatter(query_terms, 'tok', scatter_dimension=0, tiled=True)  66.6 us
    pmax x1, blocking collectives, shards(): top_all = lax.pmax(row_tops, 'tok')  56.7 us
    psum x1, blocking collectives, shards(): total_all = lax.psum(row_totals * jnp.exp(row_tops - top_all), 'tok')  52.9 us
    dot_general x16, matrix products, score_rows(): lax.dot_general(q_rows, doc_rows, (((1,), (1,)), ((), ())), preferred_ele...  30.2 us
    dot_general x8, matrix products, backward_both(): lax.dot_general(scaled, q_rows, (((0,), (0,)), ((), ())), preferred_eleme...  28.9 us
    while x32, local copies, waits for them, and re-layouts  15.2 us
    dot_general x8, matrix products, backward_both(): jnp.dot(weights_low, documents, preferred_element_type=jnp.float32)  12.4 us
  transfers between devices with their start and end apart: 2, of which 2 were waited for; matrix products, arithmetic and copies ran while one was open for 0% of the time, Pallas kernels for 0%

commit v1 on v0

--- a/solution.py
+++ b/solution.py
@@ -34,7 +34,7 @@
     row_tops = row_tops.reshape(-1)
     row_totals = row_totals.reshape(-1)
     top_all = lax.pmax(row_tops, "tok")
-    total_all = lax.psum(row_totals * jnp.exp(row_tops - top_all), "tok")
+    total_all = jnp.sum(lax.all_gather(row_totals * jnp.exp(row_tops - top_all), "tok"), axis=0)
     log_total = top_all + jnp.log(total_all)
     log_blocks = log_total.reshape(n_blocks, blk_rows)
     weight_blocks = row_weight.reshape(n_blocks, blk_rows)

time: 359 us -> 324 us (0.903)
  blocking collectives: 110 us -> 73.3 us
    psum x1 -> x0, blocking collectives: 52.9 us -> none  [shards(): total_all = lax.psum(row_totals * jnp.exp(row_tops - top_all), 'tok')]
    all_gather x0 -> x1, blocking collectives: none -> 16.7 us  [shards(): lax.all_gather(row_totals * jnp.exp(row_tops - top_all), 'tok')]
where the time goes in v1:
time: 324 us; the launch traced here: 323 us
  waiting for transfers between devices  139 us (43%)
  blocking collectives  73.3 us (23%)
  matrix products  71.5 us (22%)
  local copies, waits for them, and re-layouts  17.6 us (5%)
  between operations  14.1 us (4%)
  other arithmetic  6.66 us (2%)
    reduce_scatter x1, waiting for transfers between devices, shards(): lax.psum_scatter(doc_total, 'query', scatter_dimension=0, tiled=True)  72 us
    reduce_scatter x1, waiting for transfers between devices, shards(): lax.psum_scatter(query_terms, 'tok', scatter_dimension=0, tiled=True)  66.4 us
    pmax x1, blocking collectives, shards(): top_all = lax.pmax(row_tops, 'tok')  56.7 us
    dot_general x16, matrix products, score_rows(): lax.dot_general(q_rows, doc_rows, (((1,), (1,)), ((), ())), preferred_ele...  30.2 us
    dot_general x8, matrix products, backward_both(): lax.dot_general(scaled, q_rows, (((0,), (0,)), ((), ())), preferred_eleme...  28.9 us
    all_gather x1, blocking collectives, shards(): lax.all_gather(row_totals * jnp.exp(row_tops - top_all), 'tok')  16.7 us
    while x32, local copies, waits for them, and re-layouts  15.2 us
    dot_general x8, matrix products, backward_both(): jnp.dot(weights_low, documents, preferred_element_type=jnp.float32)  12.4 us
  transfers between devices with their start and end apart: 2, of which 2 were waited for; matrix products, arithmetic and copies ran while one was open for 0% of the time, Pallas kernels for 0%

profile of v1, /device:TPU:0, one launch (start us, length us, event | category | flops | bytes accessed | tf_op | source)
XLA Modules:
  0.0 323.2 jit_solution(4221228804349856425)
XLA Ops:
  7.3 23.1 %while.25 = (s32[]{:T(128)}, f32[8,512]{1,0:T(8,128)S(1)}, f32[8,512]{1,0:T(8,128)S(1)}, bf16[8,512,128]{2,1,0:T(8,128)(2,1)}, bf16[2048,128]{1,0:T(8,128)(2,1)}, /*index=5*/s32[]{:T(128)}, s32[]{:T(128)}) while((s32[]{:T(128)}, f32[8,512]{1,0:T(8,128)S(1)}, f32[8,512]{1,0:T(8,128)S(1)}, bf16[8,512,128]{2,1,0:T(8,128)(2,1)}, ...), condition=%wide.region_3.4_spmd, body=%wide.region_0.3_spmd.sunk | while | flops 273677312 | bytes 9058901 | solution.py:33
  7.3 1.9 multiply_reduce_fusion.2
  9.2 0.8 exponential_reduce_fusion.2
  10.1 0.1 dynamic_update_slice.16
  10.2 1.9 multiply_reduce_fusion.2
  12.1 0.8 exponential_reduce_fusion.2
  12.9 0.1 dynamic_update_slice.16
  13.0 1.9 multiply_reduce_fusion.2
  14.9 0.8 exponential_reduce_fusion.2
  15.8 0.1 dynamic_update_slice.16
  15.9 1.9 multiply_reduce_fusion.2
  17.8 0.8 exponential_reduce_fusion.2
  18.7 0.1 dynamic_update_slice.16
  18.8 1.9 multiply_reduce_fusion.2
  20.7 0.8 exponential_reduce_fusion.2
  21.7 1.9 multiply_reduce_fusion.2
  23.6 0.8 exponential_reduce_fusion.2
  24.5 0.1 dynamic_update_slice.16
  24.6 1.9 multiply_reduce_fusion.2
  26.5 0.8 exponential_reduce_fusion.2
  27.4 1.9 multiply_reduce_fusion.2
  29.4 0.8 exponential_reduce_fusion.2
  30.3 56.7 %pmax.7 = f32[4096]{0:T(1024)S(1)} all-reduce(f32[4096]{0:T(1024)S(1)} %bitcast.57), channel_id=1, replica_groups=mesh['query'=8,'tok'=16] {'tok'}, use_global_device_ids=true, to_apply=%region_4.5 | all-reduce | flops 4096 | bytes 32768 | tf_op jit(solution)/shard_map/pmax | solution.py:36
  87.0 16.7 %all-gather = f32[65536]{0:T(1024)S(1)} all-gather(f32[4096]{0:T(1024)S(1)} %exponential_multiply_fusion), channel_id=2, replica_groups=mesh['query'=8,'tok'=16] {'tok'}, dimensions={0}, use_global_device_ids=true | all-gather | bytes 278528 | tf_op jit(solution)/shard_map/all_gather | solution.py:37
  103.8 0.1 broadcast_in_dim.36
  103.9 0.1 broadcast_in_dim.37
  104.0 0.1 broadcast_in_dim.38
  104.1 72.0 %while.26 = (s32[]{:T(128)}, f32[2048,128]{1,0:T(8,128)S(1)}, f32[8,512,128]{2,1,0:T(8,128)}, f32[8,512]{1,0:T(8,128)S(1)}, bf16[8,512,128]{2,1,0:T(8,128)(2,1)}...) while((s32[]{:T(128)}, f32[2048,128]{1,0:T(8,128)S(1)}, ...), condition=%wide.region_7.8_spmd.clone, body=%wide.region_6.7_spmd.clone.sunk | while | flops 813236224 | bytes 35145376 | solution.py:56
  104.1 1.9 fusion.46
  106.0 1.9 copy-done
  107.9 1.5 fusion.47
  109.5 3.6 %convolution_add_fusion.2 = f32[2048,128]{1,0:T(8,128)S(1)} fusion(f32[512,2048]{1,0:T(8,128)} %copy-done, f32[512]{0:T(512)S(1)} %bitcast.53, f32[512]{0:T(512)S(1)} %bitcast.55, f32[2048,128]{1,0:T(8,128)S(1)} %get-tuple-element.237, pred[]{:T(512)S(6)} %compare.3, bf16[8,512,128]{2,1,0:T(8,128)(2,1)} %get-tuple-element.249, s32[]{:T(128)} %get-tuple-element.236), kind=kOutput, calls=%fused_computation.9.clone.1 | convolution fusion | flops 273154048 | bytes 6427137 | tf_op jit(solution)/shard_map/while/body/eval_jaxpr/dot_general | solution.py:51
  113.1 1.9 fusion.46
  115.0 1.9 copy-done
  116.9 1.5 fusion.47
  118.5 3.6 %convolution_add_fusion.2 = f32[2048,128]{1,0:T(8,128)S(1)} fusion(f32[512,2048]{1,0:T(8,128)} %copy-done, f32[512]{0:T(512)S(1)} %bitcast.53, f32[512]{0:T(512)S(1)} %bitcast.55, f32[2048,128]{1,0:T(8,128)S(1)} %get-tuple-element.237, pred[]{:T(512)S(6)} %compare.3, bf16[8,512,128]{2,1,0:T(8,128)(2,1)} %get-tuple-element.249, s32[]{:T(128)} %get-tuple-element.236), kind=kOutput, calls=%fused_computation.9.clone.1 | convolution fusion | flops 273154048 | bytes 6427137 | tf_op jit(solution)/shard_map/while/body/eval_jaxpr/dot_general | solution.py:51
  122.1 1.9 fusion.46
  124.0 1.9 copy-done
  125.9 1.6 fusion.47
  127.5 3.6 %convolution_add_fusion.2 = f32[2048,128]{1,0:T(8,128)S(1)} fusion(f32[512,2048]{1,0:T(8,128)} %copy-done, f32[512]{0:T(512)S(1)} %bitcast.53, f32[512]{0:T(512)S(1)} %bitcast.55, f32[2048,128]{1,0:T(8,128)S(1)} %get-tuple-element.237, pred[]{:T(512)S(6)} %compare.3, bf16[8,512,128]{2,1,0:T(8,128)(2,1)} %get-tuple-element.249, s32[]{:T(128)} %get-tuple-element.236), kind=kOutput, calls=%fused_computation.9.clone.1 | convolution fusion | flops 273154048 | bytes 6427137 | tf_op jit(solution)/shard_map/while/body/eval_jaxpr/dot_general | solution.py:51
  131.1 1.9 fusion.46
  133.0 1.9 copy-done
  134.9 1.6 fusion.47
  136.5 3.6 %convolution_add_fusion.2 = f32[2048,128]{1,0:T(8,128)S(1)} fusion(f32[512,2048]{1,0:T(8,128)} %copy-done, f32[512]{0:T(512)S(1)} %bitcast.53, f32[512]{0:T(512)S(1)} %bitcast.55, f32[2048,128]{1,0:T(8,128)S(1)} %get-tuple-element.237, pred[]{:T(512)S(6)} %compare.3, bf16[8,512,128]{2,1,0:T(8,128)(2,1)} %get-tuple-element.249, s32[]{:T(128)} %get-tuple-element.236), kind=kOutput, calls=%fused_computation.9.clone.1 | convolution fusion | flops 273154048 | bytes 6427137 | tf_op jit(solution)/shard_map/while/body/eval_jaxpr/dot_general | solution.py:51
  140.1 1.9 fusion.46
  142.0 1.9 copy-done
  143.9 1.6 fusion.47
  145.5 3.6 %convolution_add_fusion.2 = f32[2048,128]{1,0:T(8,128)S(1)} fusion(f32[512,2048]{1,0:T(8,128)} %copy-done, f32[512]{0:T(512)S(1)} %bitcast.53, f32[512]{0:T(512)S(1)} %bitcast.55, f32[2048,128]{1,0:T(8,128)S(1)} %get-tuple-element.237, pred[]{:T(512)S(6)} %compare.3, bf16[8,512,128]{2,1,0:T(8,128)(2,1)} %get-tuple-element.249, s32[]{:T(128)} %get-tuple-element.236), kind=kOutput, calls=%fused_computation.9.clone.1 | convolution fusion | flops 273154048 | bytes 6427137 | tf_op jit(solution)/shard_map/while/body/eval_jaxpr/dot_general | solution.py:51
  149.1 1.9 fusion.46
  151.0 1.9 copy-done
  152.9 1.6 fusion.47
  154.5 3.6 %convolution_add_fusion.2 = f32[2048,128]{1,0:T(8,128)S(1)} fusion(f32[512,2048]{1,0:T(8,128)} %copy-done, f32[512]{0:T(512)S(1)} %bitcast.53, f32[512]{0:T(512)S(1)} %bitcast.55, f32[2048,128]{1,0:T(8,128)S(1)} %get-tuple-element.237, pred[]{:T(512)S(6)} %compare.3, bf16[8,512,128]{2,1,0:T(8,128)(2,1)} %get-tuple-element.249, s32[]{:T(128)} %get-tuple-element.236), kind=kOutput, calls=%fused_computation.9.clone.1 | convolution fusion | flops 273154048 | bytes 6427137 | tf_op jit(solution)/shard_map/while/body/eval_jaxpr/dot_general | solution.py:51
  158.1 1.9 fusion.46
  160.0 1.9 copy-done
  161.9 1.6 fusion.47
  163.5 3.6 %convolution_add_fusion.2 = f32[2048,128]{1,0:T(8,128)S(1)} fusion(f32[512,2048]{1,0:T(8,128)} %copy-done, f32[512]{0:T(512)S(1)} %bitcast.53, f32[512]{0:T(512)S(1)} %bitcast.55, f32[2048,128]{1,0:T(8,128)S(1)} %get-tuple-element.237, pred[]{:T(512)S(6)} %compare.3, bf16[8,512,128]{2,1,0:T(8,128)(2,1)} %get-tuple-element.249, s32[]{:T(128)} %get-tuple-element.236), kind=kOutput, calls=%fused_computation.9.clone.1 | convolution fusion | flops 273154048 | bytes 6427137 | tf_op jit(solution)/shard_map/while/body/eval_jaxpr/dot_general | solution.py:51
  167.1 1.9 fusion.46
  169.0 1.9 copy-done
  170.9 1.6 fusion.47
  172.5 3.6 %convolution_add_fusion.2 = f32[2048,128]{1,0:T(8,128)S(1)} fusion(f32[512,2048]{1,0:T(8,128)} %copy-done, f32[512]{0:T(512)S(1)} %bitcast.53, f32[512]{0:T(512)S(1)} %bitcast.55, f32[2048,128]{1,0:T(8,128)S(1)} %get-tuple-element.237, pred[]{:T(512)S(6)} %compare.3, bf16[8,512,128]{2,1,0:T(8,128)(2,1)} %get-tuple-element.249, s32[]{:T(128)} %get-tuple-element.236), kind=kOutput, calls=%fused_computation.9.clone.1 | convolution fusion | flops 273154048 | bytes 6427137 | tf_op jit(solution)/shard_map/while/body/eval_jaxpr/dot_general | solution.py:51
  176.1 1.0 copy-done.2
  177.2 0.7 reduce-scatter.3.cloned.1.call-update
  177.9 72.0 %reduce-scatter.5.cloned.1.call-done = f32[256,128]{1,0:T(8,128)} async-done(((f32[2048,128]{1,0:T(8,128)}), f32[256,128]{1,0:T(8,128)}) %reduce-scatter.5.cloned.1.call-update) | async-done | bytes 131088 | tf_op jit(solution)/shard_map/reduce_scatter | solution.py:61
  249.9 66.4 %reduce-scatter.3.cloned.1.call-done = f32[256,128]{1,0:T(8,128)} async-done(((f32[4096,128]{1,0:T(8,128)}), f32[256,128]{1,0:T(8,128)}) %reduce-scatter.3.cloned.1.call-update) | async-done | bytes 131088 | tf_op jit(solution)/shard_map/reduce_scatter | solution.py:63
  (60 shorter events, 1.0 us)
Async XLA Ops:
  7.2 242.8 %reduce-scatter.5.cloned.1.call-start = ((), (), s32[]{:S(2)}) async-start(), calls=%async_computation.3 | async-start | bytes 1179648 | tf_op jit(solution)/shard_map/reduce_scatter | solution.py:61
  7.2 96.6 %copy-start.3 = (f32[128]{0:T(128)S(1)}, f32[128]{0:T(128)}, u32[]{:S(2)}) copy-start(f32[128]{0:T(128)} %param.9) | copy-start | bytes 1540
  104.1 3.8 %copy-start.1 = (bf16[2048,128]{1,0:T(8,128)(2,1)S(1)}, bf16[2048,128]{1,0:T(8,128)(2,1)}, u32[]{:S(2)}) copy-start(bf16[2048,128]{1,0:T(8,128)(2,1)} %get-tuple-element.250) | copy-start | bytes 1572868 | tf_op jit(solution)/shard_map/while
  106.0 1.9 copy-start
  113.1 3.8 %copy-start.1 = (bf16[2048,128]{1,0:T(8,128)(2,1)S(1)}, bf16[2048,128]{1,0:T(8,128)(2,1)}, u32[]{:S(2)}) copy-start(bf16[2048,128]{1,0:T(8,128)(2,1)} %get-tuple-element.250) | copy-start | bytes 1572868 | tf_op jit(solution)/shard_map/while
  115.0 1.9 copy-start
  122.1 3.8 %copy-start.1 = (bf16[2048,128]{1,0:T(8,128)(2,1)S(1)}, bf16[2048,128]{1,0:T(8,128)(2,1)}, u32[]{:S(2)}) copy-start(bf16[2048,128]{1,0:T(8,128)(2,1)} %get-tuple-element.250) | copy-start | bytes 1572868 | tf_op jit(solution)/shard_map/while
  124.0 1.9 copy-start
  131.1 3.8 %copy-start.1 = (bf16[2048,128]{1,0:T(8,128)(2,1)S(1)}, bf16[2048,128]{1,0:T(8,128)(2,1)}, u32[]{:S(2)}) copy-start(bf16[2048,128]{1,0:T(8,128)(2,1)} %get-tuple-element.250) | copy-start | bytes 1572868 | tf_op jit(solution)/shard_map/while
  133.0 1.9 copy-start
  140.1 3.8 %copy-start.1 = (bf16[2048,128]{1,0:T(8,128)(2,1)S(1)}, bf16[2048,128]{1,0:T(8,128)(2,1)}, u32[]{:S(2)}) copy-start(bf16[2048,128]{1,0:T(8,128)(2,1)} %get-tuple-element.250) | copy-start | bytes 1572868 | tf_op jit(solution)/shard_map/while
  142.0 1.9 copy-start
  149.1 3.8 %copy-start.1 = (bf16[2048,128]{1,0:T(8,128)(2,1)S(1)}, bf16[2048,128]{1,0:T(8,128)(2,1)}, u32[]{:S(2)}) copy-start(bf16[2048,128]{1,0:T(8,128)(2,1)} %get-tuple-element.250) | copy-start | bytes 1572868 | tf_op jit(solution)/shard_map/while
  151.0 1.9 copy-start
  158.1 3.8 %copy-start.1 = (bf16[2048,128]{1,0:T(8,128)(2,1)S(1)}, bf16[2048,128]{1,0:T(8,128)(2,1)}, u32[]{:S(2)}) copy-start(bf16[2048,128]{1,0:T(8,128)(2,1)} %get-tuple-element.250) | copy-start | bytes 1572868 | tf_op jit(solution)/shard_map/while
  160.0 1.9 copy-start
  167.1 3.8 %copy-start.1 = (bf16[2048,128]{1,0:T(8,128)(2,1)S(1)}, bf16[2048,128]{1,0:T(8,128)(2,1)}, u32[]{:S(2)}) copy-start(bf16[2048,128]{1,0:T(8,128)(2,1)} %get-tuple-element.250) | copy-start | bytes 1572868 | tf_op jit(solution)/shard_map/while
  169.0 1.9 copy-start
  176.1 1.0 copy-start.2
  177.1 139.2 %reduce-scatter.3.cloned.1.call-start = ((), (), s32[]{:S(2)}) async-start(), calls=%async_computation.2 | async-start | bytes 2228224 | tf_op jit(solution)/shard_map/reduce_scatter | solution.py:63
Sparse Core Ops, SparseCore 0:
  177.2 72.6 reduce-scatter.4
  252.9 63.4 reduce-scatter.2
